TPU v7x, 32 devices: a whole 2x2x4 slice. The times are simulated.
32 devices in a mesh: groups: 2 (over x), blk: 16 (over z, y, core).
Axes of the slice: x: 2, y: 2, z: 4, core: 2. Of those that a mesh axis runs over, the one named last changes fastest.
Arguments:
- hidden: bfloat16 [32, 512, 640], P(('groups', 'blk')), parts along dimension 0, may hold values from -6 to 6
- query_weight: bfloat16 [16, 2560, 640], P('blk')
- query_gain: float32 [5120], replicated, may hold values from 0.1 to 32
- frame_cache: bfloat16 [32, 2, 8, 2, 16, 640], P(('groups', 'blk')), parts along dimension 0, may hold values from -8.1 to 8.1
- span_kv: bfloat16 [32, 2, 512, 640], P(('groups', 'blk')), parts along dimension 0, may hold values from -8 to 8
- selected: int32 [4, 12], P('groups'), parts along dimension 0, may hold values from 1 to 13, as said below
- owner: int32 [4, 16], P('groups'), parts along dimension 0, may hold values from 0 to 15, each once within a row
Outputs:
- attended: bfloat16 [32, 512, 640], P(('groups', 'blk')), parts along dimension 0
There are 2 independent parts, one for each index of `groups`. A program takes and returns all parts, laid end to end along the dimension named above; an argument that names none is the same for every part. Nothing has to cross between parts.
Inputs may be any that keep to these rules, and one draw needn't show every extreme that they name: `selected`: each row names 12 different frames strictly between the first frame and the last 2; frame 16 - 3 is always among them. Each row of owner names every device of the part once, so a device keeps one frame of every rollout.
All inputs are finite; a program needn't handle non-finite values.
Results may differ from a plain program's by a relative error of at most 0.012.
The roundings to bfloat16 on the way count: a program that leaves them out, or rounds other values in their place, can miss the bound.
Values may be sent and summed in bfloat16 or wider, within the bound.
A program may use at most 64 MiB of HBM per device.

v0:
```python
import jax
import jax.numpy as jnp
from jax import lax
from jax.sharding import PartitionSpec as P

HD = 128
HG = 8
norm_epsilon = 1e-06


def from_partner(block, axis, distance):
    count = lax.axis_size(axis)
    route = []
    for low in range(count):
        high = low | 1 << distance
        if high != low and high < count:
            route += [(low, high), (high, low)]
    return lax.ppermute(block, axis, route)


def passed_along(array, axis, by):
    length = lax.axis_size(axis)
    return lax.ppermute(array, axis, [(i, (i + by) % length) for i in range(length)])


def add_columns(running, features, block_piece, offset):
    columns = lax.dynamic_slice_in_dim(features, offset, block_piece.shape[0], 1)
    return running + jnp.dot(columns, block_piece, preferred_element_type=jnp.float32)


def shards(hidden, query_weight, query_gain, frame_cache, span_kv, selected, owner):
    device = lax.axis_index("blk")
    device_count = lax.axis_size("blk")
    slot_count = device_count // HG
    slot_index = device // HG
    group_index = device % HG
    group_width = hidden.shape[2]
    bit_count = HG.bit_length() - 1
    features = hidden[0]
    for bit_number in range(bit_count):
        partner = from_partner(features, "blk", bit_number)
        upper_half = (group_index >> bit_number) % 2 == 1
        features = jnp.where(
            upper_half,
            jnp.concatenate([partner, features], 1),
            jnp.concatenate([features, partner], 1),
        )
    own_block = query_weight[0]
    block_rows = own_block.shape[0]
    running = jnp.zeros((features.shape[0], group_width), jnp.float32)
    half_rows = block_rows // 2
    first_half = own_block[:half_rows]
    second_half = own_block[half_rows:]
    running = add_columns(running, features, first_half, slot_index * block_rows)
    running = add_columns(running, features, second_half, slot_index * block_rows + half_rows)

    def turn_both(turn_index, loop_state):
        partial_sum, leading, trailing = loop_state
        leading = passed_along(leading, "blk", HG)
        trailing = passed_along(trailing, "blk", -HG)
        earlier = (slot_index - turn_index) % slot_count
        later = (slot_index + turn_index) % slot_count
        partial_sum = add_columns(partial_sum, features, leading, earlier * block_rows)
        partial_sum = add_columns(partial_sum, features, trailing, later * block_rows + half_rows)
        return (partial_sum, leading, trailing)

    running, _, _ = lax.fori_loop(1, slot_count, turn_both, (running, first_half, second_half))
    energy = jnp.sum(running * running, axis=1)
    for bit_number in range(bit_count):
        energy = energy + from_partner(energy, "blk", bit_number)
    row_scale = lax.rsqrt(energy / features.shape[1] + norm_epsilon)
    gain_slice = lax.dynamic_slice_in_dim(query_gain, group_index * group_width, group_width)
    query_rows = (running * row_scale[:, None] * gain_slice).astype(jnp.bfloat16)
    outgoing = frame_cache[0]
    outgoing = outgoing.reshape((-1,) + outgoing.shape[2:])
    incoming = lax.all_to_all(outgoing, "blk", split_axis=0, concat_axis=0, tiled=True)
    frame_count = owner.shape[1]
    window_frames = frame_count // 8
    frame_time = jnp.arange(frame_count, dtype=jnp.int32)
    chosen = (
        (frame_time == 0)
        | (frame_time >= frame_count - window_frames)
        | jnp.any(frame_time[:, None] == selected[slot_index][None, :], axis=1)
    )
    placed = owner[slot_index][:, None] == jnp.arange(device_count, dtype=jnp.int32)[None, :]
    owner_kept = jnp.any(placed & chosen[:, None], axis=0)
    frame_tokens = incoming.shape[2]
    key_rows = jnp.concatenate([incoming[:, 0].reshape(-1, group_width), span_kv[0, 0]], 0)
    value_rows = jnp.concatenate([incoming[:, 1].reshape(-1, group_width), span_kv[0, 1]], 0)
    visible = jnp.concatenate(
        [jnp.repeat(owner_kept, frame_tokens), jnp.ones((query_rows.shape[0],), dtype=bool)]
    )
    head_count = group_width // HD

    def one_head(head_index):
        start = head_index * HD
        query_part = lax.dynamic_slice_in_dim(query_rows, start, HD, 1)
        key_part = lax.dynamic_slice_in_dim(key_rows, start, HD, 1)
        value_part = lax.dynamic_slice_in_dim(value_rows, start, HD, 1)
        scores = lax.dot_general(
            query_part, key_part, (((1,), (1,)), ((), ())), preferred_element_type=jnp.float32
        ) * HD ** (-0.5)
        highest = jnp.max(jnp.where(visible, scores, -jnp.inf), axis=1, keepdims=True)
        probs = jnp.where(visible, jnp.exp(scores - highest), 0.0)
        totals = jnp.sum(probs, axis=1, keepdims=True)
        mixed_rows = jnp.dot(
            probs.astype(jnp.bfloat16), value_part, preferred_element_type=jnp.float32
        )
        return (mixed_rows / totals).astype(jnp.bfloat16)

    head_outputs = lax.map(one_head, jnp.arange(head_count, dtype=jnp.int32))
    return jnp.transpose(head_outputs, (1, 0, 2)).reshape(1, query_rows.shape[0], group_width)


def solution(mesh):
    in_specs = (
        P(("groups", "blk"), None, None),
        P("blk", None, None),
        P(),
        P(("groups", "blk"), None, None, None, None, None),
        P(("groups", "blk"), None, None, None),
        P("groups", None),
        P("groups", None),
    )
    out_specs = P(("groups", "blk"), None, None)
    return jax.shard_map(shards, mesh=mesh, in_specs=in_specs, out_specs=out_specs, check_vma=False)
```

profile of v0, /device:TPU:0, one launch (start us, length us, event | category | flops | bytes accessed | tf_op | source)
XLA Modules:
  0.0 231.8 jit_solution(16575466345846282832)
XLA Ops:
  0.5 1.9 collective-permute-done
  2.4 1.7 maximum_select_fusion.2
  4.1 3.0 %collective-permute-start.1 = (bf16[512,1280]{1,0:T(8,128)(2,1)S(1)}, bf16[512,1280]{1,0:T(8,128)(2,1)}, u32[]{:S(2)}, u32[]{:S(2)}) collective-permute-start(bf16[512,1280]{1,0:T(8,128)(2,1)S(1)} %maximum_select_fusion.2), channel_id=1, source_target_pairs={{0,2},{2,0},{1,3},{3,1},{4,6},{6,4},{5,7},{7,5},{8,10},{10,8},{9,1... | collective-permute-start | bytes 3932168 | tf_op jit(solution)/shard_map/ppermute | solution.py:18
  7.0 29.2 %collective-permute-done.1 = bf16[512,1280]{1,0:T(8,128)(2,1)} collective-permute-done((bf16[512,1280]{1,0:T(8,128)(2,1)S(1)}, bf16[512,1280]{1,0:T(8,128)(2,1)}, u32[]{:S(2)}, u32[]{:S(2)}) %collective-permute-start.1) | collective-permute-done | bytes 1310752 | tf_op jit(solution)/shard_map/ppermute | solution.py:18
  36.2 3.0 %maximum_select_fusion.1 = bf16[512,2560]{1,0:T(8,128)(2,1)S(1)} fusion(bf16[512,1280]{1,0:T(8,128)(2,1)} %copy-done.3, bf16[512,1280]{1,0:T(8,128)(2,1)} %collective-permute-done.1, pred[]{:T(512)S(6)} %eq.64), kind=kLoop, calls=%fused_computation.19 | loop fusion | flops 11796480 | bytes 5242881 | tf_op jit(solution)/shard_map/jit(_where)/select_n | solution.py:43
  39.2 1.9 collective-permute-start.2
  41.1 2.0 slice_bitcast_fusion.1
  43.1 2.6 %collective-permute-start.3 = (bf16[1280,640]{1,0:T(8,128)(2,1)}, bf16[1280,640]{1,0:T(8,128)(2,1)}, u32[]{:S(2)}, u32[]{:S(2)}) collective-permute-start(bf16[1280,640]{1,0:T(8,128)(2,1)} %get-tuple-element.80), channel_id=1, source_target_pairs={{0,8},{1,9},{2,10},{3,11},{4,12},{5,13},{6,14},{7,15},{8,0},{9,1},... | collective-permute-start | bytes 4915208 | tf_op jit(solution)/shard_map/while/body/eval_jaxpr/ppermute | solution.py:23
  46.0 4.9 %all-to-all-start = ((bf16[16,2,16,640]{3,2,1,0:T(8,128)(2,1)}), bf16[16,2,16,640]{3,2,1,0:T(8,128)(2,1)S(1)}, u32[]{:S(2)}, u32[]{:S(2)}) async-start(bf16[16,2,16,640]{3,2,1,0:T(8,128)(2,1)} %bitcast.34), calls=%async_computation | async-start | bytes 1310720 | tf_op jit(solution)/shard_map/all_to_all | solution.py:76
  51.2 2.5 %slice_bitcast_fusion.2 = (bf16[512,640]{1,0:T(8,128)(2,1)}, bf16[512,640]{1,0:T(8,128)(2,1)}) fusion(bf16[1,2,512,640]{3,2,1,0:T(8,128)(2,1)} %param.13), kind=kLoop, calls=%fused_computation.37 | loop fusion | bytes 2621440 | tf_op jit(solution)/shard_map/squeeze | solution.py:89
  53.7 99.3 %collective-permute-done.2 = bf16[512,2560]{1,0:T(8,128)(2,1)} collective-permute-done((bf16[512,2560]{1,0:T(8,128)(2,1)S(1)}, bf16[512,2560]{1,0:T(8,128)(2,1)}, u32[]{:S(2)}, u32[]{:S(2)}) %collective-permute-start.2) | collective-permute-done | bytes 2621472 | tf_op jit(solution)/shard_map/ppermute | solution.py:18
  153.0 4.5 %maximum_select_fusion = bf16[512,5120]{1,0:T(8,128)(2,1)S(1)} fusion(bf16[512,2560]{1,0:T(8,128)(2,1)S(1)} %maximum_select_fusion.1, bf16[512,2560]{1,0:T(8,128)(2,1)} %collective-permute-done.2, pred[]{:T(512)S(6)} %eq.63), kind=kLoop, calls=%fused_computation.18 | loop fusion | flops 23592960 | bytes 10485761 | tf_op jit(solution)/shard_map/jit(_where)/select_n | solution.py:43
  158.8 2.7 %fusion.18 = f32[512,640]{1,0:T(8,128)S(1)} fusion(bf16[1280,640]{1,0:T(8,128)(2,1)} %collective-permute-done.3, bf16[512,5120]{1,0:T(8,128)(2,1)S(1)} %maximum_select_fusion, s32[]{:T(128)S(6)} %select_n.106), kind=kOutput, calls=%fused_computation.30 | convolution fusion | flops 838860800 | bytes 4259844 | tf_op jit(solution)/shard_map/while/body/eval_jaxpr/dot_general | solution.py:28
  161.4 33.9 %collective-permute-done.4 = bf16[1280,640]{1,0:T(8,128)(2,1)} collective-permute-done((bf16[1280,640]{1,0:T(8,128)(2,1)}, bf16[1280,640]{1,0:T(8,128)(2,1)}, u32[]{:S(2)}, u32[]{:S(2)}) %collective-permute-start.4) | collective-permute-done | bytes 1638432 | tf_op jit(solution)/shard_map/while/body/eval_jaxpr/ppermute | solution.py:23
  195.4 2.6 %fusion.16 = f32[512,640]{1,0:T(8,128)S(1)} fusion(bf16[1280,640]{1,0:T(8,128)(2,1)} %collective-permute-done.4, bf16[512,5120]{1,0:T(8,128)(2,1)S(1)} %maximum_select_fusion, s32[]{:T(128)S(6)} %select_n.108), kind=kOutput, calls=%fused_computation.28 | convolution fusion | flops 838860800 | bytes 4259844 | tf_op jit(solution)/shard_map/while/body/eval_jaxpr/dot_general | solution.py:28
  200.5 1.5 collective-permute-start.6
  202.1 2.0 collective-permute-done.6
  204.1 2.3 pad_maximum_fusion
  207.9 21.7 %while.2 = (s32[]{:T(128)}, bf16[5,512,128]{1,2,0:T(8,128)(2,1)}, pred[768]{0:T(1024)(128)(4,1)S(1)}, s32[5]{0:T(128)S(1)}, bf16[512,640]{1,0:T(8,128)(2,1)S(1)}...) while((s32[]{:T(128)}, bf16[5,512,128]{1,2,0:T(8,128)(2,1)}, ...), condition=%wide.region_6.7_spmd, body=%wide.region_3.6_spmd.sunk | while | flops 204995584 | bytes 5912747 | solution.py:111
  210.1 1.4 fusion.42
  214.4 1.4 fusion.42
  223.1 1.4 fusion.42
  227.5 1.4 fusion.42
  229.7 2.2 copy.16
  (64 shorter events, 19.0 us)
Async XLA Ops:
  0.0 51.2 %copy-start = (s32[2,16]{1,0:T(2,128)S(1)}, s32[2,16]{1,0:T(2,128)}, u32[]{:S(2)}) copy-start(s32[2,16]{1,0:T(2,128)} %param.15) | copy-start | bytes 388
  0.0 2.4 %collective-permute-start = (bf16[512,640]{1,0:T(8,128)(2,1)}, bf16[512,640]{1,0:T(8,128)(2,1)S(1)}, u32[]{:S(2)}, u32[]{:S(2)}) collective-permute-start(bf16[512,640]{1,0:T(8,128)(2,1)} %bitcast.36), channel_id=1, source_target_pairs={{0,1},{1,0},{2,3},{3,2},{4,5},{5,4},{6,7},{7,6},{8,9},{9,8},{10,11... | collective-permute-start | bytes 1966088 | tf_op jit(solution)/shard_map/ppermute | solution.py:18
  4.1 3.0 %copy-start.3 = (bf16[512,1280]{1,0:T(8,128)(2,1)}, bf16[512,1280]{1,0:T(8,128)(2,1)S(1)}, u32[]{:S(2)}) copy-start(bf16[512,1280]{1,0:T(8,128)(2,1)S(1)} %maximum_select_fusion.2) | copy-start | bytes 3932164
  4.1 32.1 %collective-permute-start.1 = (bf16[512,1280]{1,0:T(8,128)(2,1)S(1)}, bf16[512,1280]{1,0:T(8,128)(2,1)}, u32[]{:S(2)}, u32[]{:S(2)}) collective-permute-start(bf16[512,1280]{1,0:T(8,128)(2,1)S(1)} %maximum_select_fusion.2), channel_id=1, source_target_pairs={{0,2},{2,0},{1,3},{3,1},{4,6},{6,4},{5,7},{7,5},{8,10},{10,8},{9,1... | collective-permute-start | bytes 3932168 | tf_op jit(solution)/shard_map/ppermute | solution.py:18
  7.0 34.0 %copy-start.1 = (bf16[1,2560,640]{2,1,0:T(8,128)(2,1)S(1)}, bf16[1,2560,640]{2,1,0:T(8,128)(2,1)}, u32[]{:S(2)}) copy-start(bf16[1,2560,640]{2,1,0:T(8,128)(2,1)} %param.10) | copy-start | bytes 9830404
  39.2 11.8 %copy-start.5 = (s32[2,12]{1,0:T(2,128)S(1)}, s32[2,12]{1,0:T(2,128)}, u32[]{:S(2)}) copy-start(s32[2,12]{1,0:T(2,128)} %param.14) | copy-start | bytes 292
  39.2 113.8 %collective-permute-start.2 = (bf16[512,2560]{1,0:T(8,128)(2,1)S(1)}, bf16[512,2560]{1,0:T(8,128)(2,1)}, u32[]{:S(2)}, u32[]{:S(2)}) collective-permute-start(bf16[512,2560]{1,0:T(8,128)(2,1)S(1)} %maximum_select_fusion.1), channel_id=1, source_target_pairs={{0,4},{4,0},{1,5},{5,1},{2,6},{6,2},{3,7},{7,3},{8,12},{12,8},{9,1... | collective-permute-start | bytes 7864328 | tf_op jit(solution)/shard_map/ppermute | solution.py:18
  43.1 115.7 %collective-permute-start.3 = (bf16[1280,640]{1,0:T(8,128)(2,1)}, bf16[1280,640]{1,0:T(8,128)(2,1)}, u32[]{:S(2)}, u32[]{:S(2)}) collective-permute-start(bf16[1280,640]{1,0:T(8,128)(2,1)} %get-tuple-element.80), channel_id=1, source_target_pairs={{0,8},{1,9},{2,10},{3,11},{4,12},{5,13},{6,14},{7,15},{8,0},{9,1},... | collective-permute-start | bytes 4915208 | tf_op jit(solution)/shard_map/while/body/eval_jaxpr/ppermute | solution.py:23
  45.6 149.7 %collective-permute-start.4 = (bf16[1280,640]{1,0:T(8,128)(2,1)}, bf16[1280,640]{1,0:T(8,128)(2,1)}, u32[]{:S(2)}, u32[]{:S(2)}) collective-permute-start(bf16[1280,640]{1,0:T(8,128)(2,1)} %get-tuple-element.81), channel_id=1, source_target_pairs={{0,8},{1,9},{2,10},{3,11},{4,12},{5,13},{6,14},{7,15},{8,0},{9,1},... | collective-permute-start | bytes 4915208 | tf_op jit(solution)/shard_map/while/body/eval_jaxpr/ppermute | solution.py:23
  46.0 156.1 %all-to-all-start = ((bf16[16,2,16,640]{3,2,1,0:T(8,128)(2,1)}), bf16[16,2,16,640]{3,2,1,0:T(8,128)(2,1)S(1)}, u32[]{:S(2)}, u32[]{:S(2)}) async-start(bf16[16,2,16,640]{3,2,1,0:T(8,128)(2,1)} %bitcast.34), calls=%async_computation | async-start | bytes 1310720 | tf_op jit(solution)/shard_map/all_to_all | solution.py:76
  53.7 103.9 %copy-start.2 = (bf16[1,2560,640]{2,1,0:T(8,128)(2,1)S(1)}, bf16[1,2560,640]{2,1,0:T(8,128)(2,1)}, u32[]{:S(2)}) copy-start(bf16[1,2560,640]{2,1,0:T(8,128)(2,1)} %param.10) | copy-start | bytes 9830404
  199.3 4.8 %copy-start.4 = (bf16[512,640]{1,0:T(8,128)(2,1)S(1)}, bf16[512,640]{1,0:T(8,128)(2,1)}, u32[]{:S(2)}) copy-start(bf16[512,640]{1,0:T(8,128)(2,1)} %get-tuple-element.82) | copy-start | bytes 1966084
  199.3 1.2 collective-permute-start.5
  200.5 3.6 %collective-permute-start.6 = (f32[512]{0:T(512)S(1)}, f32[512]{0:T(512)S(1)}, u32[]{:S(2)}, u32[]{:S(2)}) collective-permute-start(f32[512]{0:T(512)S(1)} %add.114), channel_id=1, source_target_pairs={{0,2},{2,0},{1,3},{3,1},{4,6},{6,4},{5,7},{7,5},{8,10},{10,8},{9,1... | collective-permute-start | bytes 6152 | tf_op jit(solution)/shard_map/ppermute | solution.py:18
  204.1 3.6 %collective-permute-start.7 = (f32[512]{0:T(512)S(1)}, f32[512]{0:T(512)S(1)}, u32[]{:S(2)}, u32[]{:S(2)}) collective-permute-start(f32[512]{0:T(512)S(1)} %add.115), channel_id=1, source_target_pairs={{0,4},{4,0},{1,5},{5,1},{2,6},{6,2},{3,7},{7,3},{8,12},{12,8},{9,1... | collective-permute-start | bytes 6152 | tf_op jit(solution)/shard_map/ppermute | solution.py:18
where the time goes:
time: 232 us
  waiting for transfers between devices  168 us (72%)
  matrix products  17.2 us (7%)
  starting transfers between devices  14.7 us (6%)
  local copies, waits for them, and re-layouts  14.5 us (6%)
  other arithmetic  14.1 us (6%)
  loops' own time  3.36 us (1%)
    ppermute x6, waiting for transfers between devices, from_partner(): return lax.ppermute(block, axis, route)  134 us
    ppermute x2, waiting for transfers between devices, passed_along(): lax.ppermute(array, axis, [(i, (i + by) % length) for i in range(length)])  33.9 us
    select_n x3, other arithmetic, shards(): jnp.where(upper_half, jnp.concatenate([partner, features], 1), jnp.concat...  9.16 us
    dot_general x4, matrix products, add_columns(): jnp.dot(columns, block_piece, preferred_element_type=jnp.float32)  7.81 us
    dot_general x5, matrix products, one_head(): jnp.dot(probs.astype(jnp.bfloat16), value_part, preferred_element_type=jn...  7.09 us
    ppermute x6, starting transfers between devices, from_partner(): return lax.ppermute(block, axis, route)  6.86 us
    all_to_all x1, starting transfers between devices, shards(): lax.all_to_all(outgoing, 'blk', split_axis=0, concat_axis=0, tiled=True)  4.93 us
  transfers between devices with their start and end apart: 9, of which 7 were waited for; matrix products, arithmetic and copies ran while one was open for 9% of the time, Pallas kernels for 0%

commit v1 on v0

--- a/solution.py
+++ b/solution.py
@@ -6,6 +6,28 @@
 HD = 128
 HG = 8
 norm_epsilon = 1e-06
+
+
+def in_blocks(x, dim, size):
+    before, after = (x.shape[:dim], x.shape[dim + 1 :])
+    return jnp.moveaxis(x.reshape(*before, size, -1, *after), dim, 0)
+
+
+def laid_out(blocks, dim):
+    blocks = jnp.moveaxis(blocks, 0, dim)
+    shape = blocks.shape
+    return blocks.reshape(*shape[:dim], shape[dim] * shape[dim + 1], *shape[dim + 2 :])
+
+
+def pairwise_exchange(x, axis, split_dim, concat_dim):
+    peers, here = (lax.axis_size(axis), lax.axis_index(axis))
+    parts = in_blocks(x, split_dim, peers)
+    outs = [parts[here]]
+    for turn in range(1, peers):
+        sent = parts[here ^ turn]
+        outs.append(lax.ppermute(sent, axis, [(i, i ^ turn) for i in range(peers)]))
+    parts = jnp.stack(outs)[here ^ jnp.arange(peers)]
+    return laid_out(parts, concat_dim)
 
 
 def from_partner(block, axis, distance):
@@ -73,7 +95,7 @@
     query_rows = (running * row_scale[:, None] * gain_slice).astype(jnp.bfloat16)
     outgoing = frame_cache[0]
     outgoing = outgoing.reshape((-1,) + outgoing.shape[2:])
-    incoming = lax.all_to_all(outgoing, "blk", split_axis=0, concat_axis=0, tiled=True)
+    incoming = pairwise_exchange(outgoing, "blk", 0, 0)
     frame_count = owner.shape[1]
     window_frames = frame_count // 8
     frame_time = jnp.arange(frame_count, dtype=jnp.int32)

time: 232 us -> 293 us (1.26)
  waiting for transfers between devices: 168 us -> 213 us
  starting transfers between devices: 14.7 us -> 28.2 us
  local copies, waits for them, and re-layouts: 14.5 us -> 27 us
  matrix products: 17.2 us -> 10.7 us
  other arithmetic: 14.1 us -> 10.7 us
    ppermute x6, waiting for transfers between devices: 134 us -> 29.9 us  [from_partner(): return lax.ppermute(block, axis, route)]
    ppermute x2, waiting for transfers between devices: 33.9 us -> 135 us  [passed_along(): lax.ppermute(array, axis, [(i, (i + by) % length) for i in range(length)])]
    ppermute x0 -> x15, waiting for transfers between devices: none -> 47.3 us  [pairwise_exchange(): outs.append(lax.ppermute(sent, axis, [(i, i ^ turn) for i in range(peers)]))]
    ppermute x0 -> x15, starting transfers between devices: none -> 21.7 us  [pairwise_exchange(): outs.append(lax.ppermute(sent, axis, [(i, i ^ turn) for i in range(peers)]))]
    unnamed x12 -> x34, local copies, waits for them, and re-layouts: 0.03 us -> 11.7 us
    all_to_all x1 -> x0, starting transfers between devices: 4.93 us -> none  [shards(): lax.all_to_all(outgoing, 'blk', split_axis=0, concat_axis=0, tiled=True)]
    dot_general x5, matrix products: 7.09 us -> 2.48 us  [one_head(): jnp.dot(probs.astype(jnp.bfloat16), value_part, preferred_element_type=jn...]
    ppermute x6, starting transfers between devices: 6.86 us -> 3.56 us  [from_partner(): return lax.ppermute(block, axis, route)]
  transfers between devices with their start and end apart: 9 -> 23, of which waited for: 7 -> 6; matrix products, arithmetic and copies ran while one was open for 9% -> 12% of each run, Pallas kernels for 0% -> 0%
where the time goes in v1:
time: 293 us
  waiting for transfers between devices  213 us (73%)
  starting transfers between devices  28.2 us (10%)
  local copies, waits for them, and re-layouts  27 us (9%)
  other arithmetic  10.7 us (4%)
  matrix products  10.7 us (4%)
  loops' own time  3.46 us (1%)
    ppermute x2, waiting for transfers between devices, passed_along(): lax.ppermute(array, axis, [(i, (i + by) % length) for i in range(length)])  135 us
    ppermute x15, waiting for transfers between devices, pairwise_exchange(): outs.append(lax.ppermute(sent, axis, [(i, i ^ turn) for i in range(peers)]))  47.3 us
    ppermute x6, waiting for transfers between devices, from_partner(): return lax.ppermute(block, axis, route)  29.9 us
    ppermute x15, starting transfers between devices, pairwise_exchange(): outs.append(lax.ppermute(sent, axis, [(i, i ^ turn) for i in range(peers)]))  21.7 us
    unnamed x34, local copies, waits for them, and re-layouts  11.7 us
    select_n x3, other arithmetic, shards(): jnp.where(upper_half, jnp.concatenate([partner, features], 1), jnp.concat...  7.86 us
    dot_general x4, matrix products, add_columns(): jnp.dot(columns, block_piece, preferred_element_type=jnp.float32)  5.98 us
  transfers between devices with their start and end apart: 23, of which 6 were waited for; matrix products, arithmetic and copies ran while one was open for 12% of the time, Pallas kernels for 0%

profile of v1, /device:TPU:0, one launch (start us, length us, event | category | flops | bytes accessed | tf_op | source)
XLA Modules:
  0.0 292.7 jit_solution(7524180392895516464)
XLA Ops:
  0.0 1.9 dynamic-slice_bitcast_fusion
  2.4 2.6 collective-permute-start.9
  5.1 1.8 collective-permute-start.11
  7.9 2.6 slice_bitcast_fusion.2
  10.5 3.1 %maximum_select_fusion.2 = bf16[512,1280]{1,0:T(8,128)(2,1)} fusion(bf16[512,640]{1,0:T(8,128)(2,1)} %bitcast.101, bf16[512,640]{1,0:T(8,128)(2,1)} %collective-permute-done, pred[]{:T(512)S(6)} %eq.65), kind=kLoop, calls=%fused_computation.26 | loop fusion | flops 5898240 | bytes 2621441 | tf_op jit(solution)/shard_map/jit(_where)/select_n | solution.py:65
  15.1 2.0 slice_bitcast_fusion.1
  22.6 23.3 %collective-permute-done.1 = bf16[512,1280]{1,0:T(8,128)(2,1)} collective-permute-done((bf16[512,1280]{1,0:T(8,128)(2,1)}, bf16[512,1280]{1,0:T(8,128)(2,1)}, u32[]{:S(2)}, u32[]{:S(2)}) %collective-permute-start.1) | collective-permute-done | bytes 1310752 | tf_op jit(solution)/shard_map/ppermute | solution.py:40
  46.7 3.2 %maximum_select_fusion.1 = bf16[512,2560]{1,0:T(8,128)(2,1)S(1)} fusion(bf16[512,1280]{1,0:T(8,128)(2,1)} %maximum_select_fusion.2, bf16[512,1280]{1,0:T(8,128)(2,1)} %collective-permute-done.1, pred[]{:T(512)S(6)} %eq.64), kind=kLoop, calls=%fused_computation.20 | loop fusion | flops 11796480 | bytes 5242881 | tf_op jit(solution)/shard_map/jit(_where)/select_n | solution.py:65
  49.9 1.6 collective-permute-start.2
  52.9 2.6 collective-permute-start.15
  57.8 2.5 collective-permute-start.17
  62.4 47.3 %collective-permute-done.15 = bf16[1,2,16,640]{3,2,1,0:T(8,128)(2,1)S(1)} collective-permute-done((bf16[1,2,16,640]{3,2,1,0:T(8,128)(2,1)S(1)}, bf16[1,2,16,640]{3,2,1,0:T(8,128)(2,1)S(1)}, u32[]{:S(2)}, u32[]{:S(2)}) %collective-permute-start.15) | collective-permute-done | bytes 40992 | tf_op jit(solution)/shard_map/ppermute | solution.py:28
  109.7 2.5 collective-permute-start.19
  113.9 2.1 collective-permute-start.21
  116.7 2.8 collective-permute-start.22
  120.8 2.9 collective-permute-start.4
  124.9 1.6 maximum_select_fusion
  127.7 101.5 %collective-permute-done.3 = bf16[1280,640]{1,0:T(8,128)(2,1)S(1)} collective-permute-done((bf16[1280,640]{1,0:T(8,128)(2,1)S(1)}, bf16[1280,640]{1,0:T(8,128)(2,1)S(1)}, u32[]{:S(2)}, u32[]{:S(2)}) %collective-permute-start.3) | collective-permute-done | bytes 1638432 | tf_op jit(solution)/shard_map/while/body/eval_jaxpr/ppermute | solution.py:45
  230.4 33.8 %collective-permute-done.4 = bf16[1280,640]{1,0:T(8,128)(2,1)S(1)} collective-permute-done((bf16[1280,640]{1,0:T(8,128)(2,1)S(1)}, bf16[1280,640]{1,0:T(8,128)(2,1)S(1)}, u32[]{:S(2)}, u32[]{:S(2)}) %collective-permute-start.4) | collective-permute-done | bytes 1638432 | tf_op jit(solution)/shard_map/while/body/eval_jaxpr/ppermute | solution.py:45
  265.4 2.3 multiply_reduce_fusion
  268.4 1.7 gather_fusion
  270.6 3.3 %collective-permute-done.6 = f32[512]{0:T(512)S(1)} collective-permute-done((f32[512]{0:T(512)S(1)}, f32[512]{0:T(512)S(1)}, u32[]{:S(2)}, u32[]{:S(2)}) %collective-permute-start.6) | collective-permute-done | bytes 2080 | tf_op jit(solution)/shard_map/ppermute | solution.py:40
  274.1 3.4 %collective-permute-done.7 = f32[512]{0:T(512)S(1)} collective-permute-done((f32[512]{0:T(512)S(1)}, f32[512]{0:T(512)S(1)}, u32[]{:S(2)}, u32[]{:S(2)}) %collective-permute-start.7) | collective-permute-done | bytes 2080 | tf_op jit(solution)/shard_map/ppermute | solution.py:40
  277.7 14.0 %while.2 = (s32[]{:T(128)}, bf16[5,512,128]{1,2,0:T(8,128)(2,1)S(1)}, pred[768]{0:T(1024)(128)(4,1)S(1)}, s32[5]{0:T(128)S(1)}, bf16[512,640]{1,0:T(8,128)(2,1)S...) while((s32[]{:T(128)}, ...), condition=%wide.region_6.7_spmd, body=%wide.region_3.6_spmd.sunk | while | flops 204995584 | bytes 5912495 | solution.py:133
  (119 shorter events, 36.6 us)
Async XLA Ops:
  1.9 16.2 %collective-permute-start.8 = (bf16[1,2,16,640]{3,2,1,0:T(8,128)(2,1)}, bf16[1,2,16,640]{3,2,1,0:T(8,128)(2,1)}, u32[]{:S(2)}, u32[]{:S(2)}) collective-permute-start(bf16[1,2,16,640]{3,2,1,0:T(8,128)(2,1)} %get-tuple-element.100), channel_id=1, source_target_pairs={{0,1},{1,0},{2,3},{3,2},{4,5},{5,4},{6,7},{7,6},{8,9},{9,8},{10,11... | collective-permute-start | bytes 122888 | tf_op jit(solution)/shard_map/ppermute | solution.py:28
  2.4 17.3 %collective-permute-start.9 = (bf16[1,2,16,640]{3,2,1,0:T(8,128)(2,1)}, bf16[1,2,16,640]{3,2,1,0:T(8,128)(2,1)}, u32[]{:S(2)}, u32[]{:S(2)}) collective-permute-start(bf16[1,2,16,640]{3,2,1,0:T(8,128)(2,1)} %get-tuple-element.99), channel_id=1, source_target_pairs={{0,2},{1,3},{2,0},{3,1},{4,6},{5,7},{6,4},{7,5},{8,10},{9,11},{10,... | collective-permute-start | bytes 122888 | tf_op jit(solution)/shard_map/ppermute | solution.py:28
  5.0 44.9 %collective-permute-start.10 = (bf16[1,2,16,640]{3,2,1,0:T(8,128)(2,1)}, bf16[1,2,16,640]{3,2,1,0:T(8,128)(2,1)}, u32[]{:S(2)}, u32[]{:S(2)}) collective-permute-start(bf16[1,2,16,640]{3,2,1,0:T(8,128)(2,1)} %get-tuple-element.98), channel_id=1, source_target_pairs={{0,3},{1,2},{2,1},{3,0},{4,7},{5,6},{6,5},{7,4},{8,11},{9,10},{10,... | collective-permute-start | bytes 122888 | tf_op jit(solution)/shard_map/ppermute | solution.py:28
  5.1 47.8 %collective-permute-start.11 = (bf16[1,2,16,640]{3,2,1,0:T(8,128)(2,1)}, bf16[1,2,16,640]{3,2,1,0:T(8,128)(2,1)}, u32[]{:S(2)}, u32[]{:S(2)}) collective-permute-start(bf16[1,2,16,640]{3,2,1,0:T(8,128)(2,1)} %get-tuple-element.97), channel_id=1, source_target_pairs={{0,4},{1,5},{2,6},{3,7},{4,0},{5,1},{6,2},{7,3},{8,12},{9,13},{10,... | collective-permute-start | bytes 122888 | tf_op jit(solution)/shard_map/ppermute | solution.py:28
  6.9 3.7 %collective-permute-start = (bf16[512,640]{1,0:T(8,128)(2,1)}, bf16[512,640]{1,0:T(8,128)(2,1)}, u32[]{:S(2)}, u32[]{:S(2)}) collective-permute-start(bf16[512,640]{1,0:T(8,128)(2,1)} %bitcast.100), channel_id=1, source_target_pairs={{0,1},{1,0},{2,3},{3,2},{4,5},{5,4},{6,7},{7,6},{8,9},{9,8},{10,11... | collective-permute-start | bytes 1966088 | tf_op jit(solution)/shard_map/ppermute | solution.py:40
  13.6 32.3 %collective-permute-start.1 = (bf16[512,1280]{1,0:T(8,128)(2,1)}, bf16[512,1280]{1,0:T(8,128)(2,1)}, u32[]{:S(2)}, u32[]{:S(2)}) collective-permute-start(bf16[512,1280]{1,0:T(8,128)(2,1)} %maximum_select_fusion.2), channel_id=1, source_target_pairs={{0,2},{2,0},{1,3},{3,1},{4,6},{6,4},{5,7},{7,5},{8,10},{10,8},{9,1... | collective-permute-start | bytes 3932168 | tf_op jit(solution)/shard_map/ppermute | solution.py:40
  18.1 38.8 %collective-permute-start.12 = (bf16[1,2,16,640]{3,2,1,0:T(8,128)(2,1)}, bf16[1,2,16,640]{3,2,1,0:T(8,128)(2,1)S(1)}, u32[]{:S(2)}, u32[]{:S(2)}) collective-permute-start(bf16[1,2,16,640]{3,2,1,0:T(8,128)(2,1)} %get-tuple-element.96), channel_id=1, source_target_pairs={{0,5},{1,4},{2,7},{3,6},{4,1},{5,0},{6,3},{7,2},{8,13},{9,12},{10,... | collective-permute-start | bytes 122888 | tf_op jit(solution)/shard_map/ppermute | solution.py:28
  19.7 38.0 %collective-permute-start.13 = (bf16[1,2,16,640]{3,2,1,0:T(8,128)(2,1)}, bf16[1,2,16,640]{3,2,1,0:T(8,128)(2,1)S(1)}, u32[]{:S(2)}, u32[]{:S(2)}) collective-permute-start(bf16[1,2,16,640]{3,2,1,0:T(8,128)(2,1)} %get-tuple-element.95), channel_id=1, source_target_pairs={{0,6},{1,7},{2,4},{3,5},{4,2},{5,3},{6,0},{7,1},{8,14},{9,15},{10,... | collective-permute-start | bytes 122888 | tf_op jit(solution)/shard_map/ppermute | solution.py:28
  45.9 74.8 %copy-start.5 = (bf16[1280,640]{1,0:T(8,128)(2,1)S(1)}, bf16[1280,640]{1,0:T(8,128)(2,1)}, u32[]{:S(2)}) copy-start(bf16[1280,640]{1,0:T(8,128)(2,1)} %get-tuple-element.81) | copy-start | bytes 4915204
  45.9 15.0 %collective-permute-start.14 = (bf16[1,2,16,640]{3,2,1,0:T(8,128)(2,1)}, bf16[1,2,16,640]{3,2,1,0:T(8,128)(2,1)S(1)}, u32[]{:S(2)}, u32[]{:S(2)}) collective-permute-start(bf16[1,2,16,640]{3,2,1,0:T(8,128)(2,1)} %get-tuple-element.94), channel_id=1, source_target_pairs={{0,7},{1,6},{2,5},{3,4},{4,3},{5,2},{6,1},{7,0},{8,15},{9,14},{10,... | collective-permute-start | bytes 122888 | tf_op jit(solution)/shard_map/ppermute | solution.py:28
  49.9 75.0 %collective-permute-start.2 = (bf16[512,2560]{1,0:T(8,128)(2,1)S(1)}, bf16[512,2560]{1,0:T(8,128)(2,1)S(1)}, u32[]{:S(2)}, u32[]{:S(2)}) collective-permute-start(bf16[512,2560]{1,0:T(8,128)(2,1)S(1)} %maximum_select_fusion.1), channel_id=1, source_target_pairs={{0,4},{4,0},{1,5},{5,1},{2,6},{6,2},{3,7},{7,3},{8,12},{12,8},{9,1... | collective-permute-start | bytes 7864328 | tf_op jit(solution)/shard_map/ppermute | solution.py:40
  52.9 56.7 %collective-permute-start.15 = (bf16[1,2,16,640]{3,2,1,0:T(8,128)(2,1)S(1)}, bf16[1,2,16,640]{3,2,1,0:T(8,128)(2,1)S(1)}, u32[]{:S(2)}, u32[]{:S(2)}) collective-permute-start(bf16[1,2,16,640]{3,2,1,0:T(8,128)(2,1)S(1)} %copy-done.9), channel_id=1, source_target_pairs={{0,8},{1,9},{2,10},{3,11},{4,12},{5,13},{6,14},{7,15},{8,0},{9,1},... | collective-permute-start | bytes 122888 | tf_op jit(solution)/shard_map/ppermute | solution.py:28
  56.9 55.9 %collective-permute-start.16 = (bf16[1,2,16,640]{3,2,1,0:T(8,128)(2,1)S(1)}, bf16[1,2,16,640]{3,2,1,0:T(8,128)(2,1)S(1)}, u32[]{:S(2)}, u32[]{:S(2)}) collective-permute-start(bf16[1,2,16,640]{3,2,1,0:T(8,128)(2,1)S(1)} %copy-done.8), channel_id=1, source_target_pairs={{0,9},{1,8},{2,11},{3,10},{4,13},{5,12},{6,15},{7,14},{8,1},{9,0},... | collective-permute-start | bytes 122888 | tf_op jit(solution)/shard_map/ppermute | solution.py:28
  57.8 56.2 %collective-permute-start.17 = (bf16[1,2,16,640]{3,2,1,0:T(8,128)(2,1)S(1)}, bf16[1,2,16,640]{3,2,1,0:T(8,128)(2,1)S(1)}, u32[]{:S(2)}, u32[]{:S(2)}) collective-permute-start(bf16[1,2,16,640]{3,2,1,0:T(8,128)(2,1)S(1)} %get-tuple-element.91), channel_id=1, source_target_pairs={{0,10},{1,11},{2,8},{3,9},{4,14},{5,15},{6,12},{7,13},{8,2},{9,3},... | collective-permute-start | bytes 122888 | tf_op jit(solution)/shard_map/ppermute | solution.py:28
  60.9 55.8 %collective-permute-start.18 = (bf16[1,2,16,640]{3,2,1,0:T(8,128)(2,1)S(1)}, bf16[1,2,16,640]{3,2,1,0:T(8,128)(2,1)S(1)}, u32[]{:S(2)}, u32[]{:S(2)}) collective-permute-start(bf16[1,2,16,640]{3,2,1,0:T(8,128)(2,1)S(1)} %get-tuple-element.90), channel_id=1, source_target_pairs={{0,11},{1,10},{2,9},{3,8},{4,15},{5,14},{6,13},{7,12},{8,3},{9,2},... | collective-permute-start | bytes 122888 | tf_op jit(solution)/shard_map/ppermute | solution.py:28
  109.7 10.5 %collective-permute-start.19 = (bf16[1,2,16,640]{3,2,1,0:T(8,128)(2,1)S(1)}, bf16[1,2,16,640]{3,2,1,0:T(8,128)(2,1)S(1)}, u32[]{:S(2)}, u32[]{:S(2)}) collective-permute-start(bf16[1,2,16,640]{3,2,1,0:T(8,128)(2,1)S(1)} %get-tuple-element.89), channel_id=1, source_target_pairs={{0,12},{1,13},{2,14},{3,15},{4,8},{5,9},{6,10},{7,11},{8,4},{9,5},... | collective-permute-start | bytes 122888 | tf_op jit(solution)/shard_map/ppermute | solution.py:28
  112.8 8.0 %collective-permute-start.20 = (bf16[1,2,16,640]{3,2,1,0:T(8,128)(2,1)S(1)}, bf16[1,2,16,640]{3,2,1,0:T(8,128)(2,1)S(1)}, u32[]{:S(2)}, u32[]{:S(2)}) collective-permute-start(bf16[1,2,16,640]{3,2,1,0:T(8,128)(2,1)S(1)} %get-tuple-element.88), channel_id=1, source_target_pairs={{0,13},{1,12},{2,15},{3,14},{4,9},{5,8},{6,11},{7,10},{8,5},{9,4},... | collective-permute-start | bytes 122888 | tf_op jit(solution)/shard_map/ppermute | solution.py:28
  113.9 10.4 %collective-permute-start.21 = (bf16[1,2,16,640]{3,2,1,0:T(8,128)(2,1)S(1)}, bf16[1,2,16,640]{3,2,1,0:T(8,128)(2,1)S(1)}, u32[]{:S(2)}, u32[]{:S(2)}) collective-permute-start(bf16[1,2,16,640]{3,2,1,0:T(8,128)(2,1)S(1)} %get-tuple-element.87), channel_id=1, source_target_pairs={{0,14},{1,15},{2,12},{3,13},{4,10},{5,11},{6,8},{7,9},{8,6},{9,7},... | collective-permute-start | bytes 122888 | tf_op jit(solution)/shard_map/ppermute | solution.py:28
  116.7 151.1 %collective-permute-start.22 = (bf16[1,2,16,640]{3,2,1,0:T(8,128)(2,1)S(1)}, bf16[1,2,16,640]{3,2,1,0:T(8,128)(2,1)S(1)}, u32[]{:S(2)}, u32[]{:S(2)}) collective-permute-start(bf16[1,2,16,640]{3,2,1,0:T(8,128)(2,1)S(1)} %get-tuple-element.86), channel_id=1, source_target_pairs={{0,15},{1,14},{2,13},{3,12},{4,11},{5,10},{6,9},{7,8},{8,7},{9,6},... | collective-permute-start | bytes 122888 | tf_op jit(solution)/shard_map/ppermute | solution.py:28
  120.1 109.1 %collective-permute-start.3 = (bf16[1280,640]{1,0:T(8,128)(2,1)S(1)}, bf16[1280,640]{1,0:T(8,128)(2,1)S(1)}, u32[]{:S(2)}, u32[]{:S(2)}) collective-permute-start(bf16[1280,640]{1,0:T(8,128)(2,1)S(1)} %copy-done.6), channel_id=1, source_target_pairs={{0,8},{1,9},{2,10},{3,11},{4,12},{5,13},{6,14},{7,15},{8,0},{9,1},... | collective-permute-start | bytes 4915208 | tf_op jit(solution)/shard_map/while/body/eval_jaxpr/ppermute | solution.py:45
  120.8 143.4 %collective-permute-start.4 = (bf16[1280,640]{1,0:T(8,128)(2,1)S(1)}, bf16[1280,640]{1,0:T(8,128)(2,1)S(1)}, u32[]{:S(2)}, u32[]{:S(2)}) collective-permute-start(bf16[1280,640]{1,0:T(8,128)(2,1)S(1)} %copy-done.5), channel_id=1, source_target_pairs={{0,8},{1,9},{2,10},{3,11},{4,12},{5,13},{6,14},{7,15},{8,0},{9,1},... | collective-permute-start | bytes 4915208 | tf_op jit(solution)/shard_map/while/body/eval_jaxpr/ppermute | solution.py:45
  267.8 2.4 collective-permute-start.5
  270.2 3.7 %collective-permute-start.6 = (f32[512]{0:T(512)S(1)}, f32[512]{0:T(512)S(1)}, u32[]{:S(2)}, u32[]{:S(2)}) collective-permute-start(f32[512]{0:T(512)S(1)} %add.172), channel_id=1, source_target_pairs={{0,2},{2,0},{1,3},{3,1},{4,6},{6,4},{5,7},{7,5},{8,10},{10,8},{9,1... | collective-permute-start | bytes 6152 | tf_op jit(solution)/shard_map/ppermute | solution.py:40
  273.9 3.6 %collective-permute-start.7 = (f32[512]{0:T(512)S(1)}, f32[512]{0:T(512)S(1)}, u32[]{:S(2)}, u32[]{:S(2)}) collective-permute-start(f32[512]{0:T(512)S(1)} %add.173), channel_id=1, source_target_pairs={{0,4},{4,0},{1,5},{5,1},{2,6},{6,2},{3,7},{7,3},{8,12},{12,8},{9,1... | collective-permute-start | bytes 6152 | tf_op jit(solution)/shard_map/ppermute | solution.py:40
  (9 other events, 126.5 us)
